TPU v7x, 512 devices: a whole 4x8x8 slice. The times are simulated.
512 devices in a mesh: dop: 16 (over z, core), rng: 32 (over x, y).
Axes of the slice: x: 4, y: 8, z: 8, core: 2. Of those that a mesh axis runs over, the one named last changes fastest.
Arguments:
- cube: bfloat16 [2, 64, 128, 16384], P(None, None, 'dop', 'rng'), may hold values from -200 to 200
- train_blocks: int32 [128, 128], P('dop', 'rng'), may hold values 0 or 1
- guard_blocks: int32 [128], P('rng'), may hold values 0 or 1
- prior_factor: float32 [128, 256, 256], P('dop', 'rng'), may hold values from -1638400 to 1638400, as said below
- steering: float32 [128, 256], P('dop'), may hold values from -6 to 6
Outputs:
- filtered: float32 [2, 128, 16384], P(None, 'dop', 'rng')
- factor: float32 [128, 256, 256], P('dop', 'rng')
Inputs may be any that keep to these rules, and one draw needn't show every extreme that they name: `prior_factor`: upper triangular with a positive diagonal.
All inputs are finite; a program needn't handle non-finite values. No bound on the sum of `train_blocks` or of `guard_blocks` on one device may be relied on, other than what follows from the above.
Results may differ from a plain program's by a relative error of at most 0.0041.
Values may be sent and summed in bfloat16 or wider, within the bound.
A program may use at most 64 MiB of HBM per device.

v0:
```python
import math
import jax
import jax.numpy as jnp
from jax import lax
from jax.sharding import PartitionSpec as P

BLOCK = 128
forgetting = 0.98


def from_behind(block, axis, distance):
    devices = range(lax.axis_size(axis))
    route = [((i - distance) % len(devices), i) for i in devices]
    return lax.ppermute(block, axis, route)


def dft_table(pulses):
    index = jnp.arange(pulses, dtype=jnp.int32)
    product = index[:, None] * index[None, :] % pulses
    angle = product.astype(jnp.float32) * (2.0 * math.pi / pulses)
    cosine = jnp.cos(angle)
    sine = jnp.sin(angle)
    top = jnp.stack([cosine, -sine], axis=1)
    bottom = jnp.stack([sine, cosine], axis=1)
    return jnp.stack([top, bottom], axis=0)


def spectra(pulse_block, table):
    out = jnp.einsum(
        "scpg,sptk->tckg", pulse_block.astype(jnp.float32), table, precision=lax.Precision.HIGHEST
    )
    return out.astype(jnp.bfloat16)


def shards(cube, train_blocks, guard_blocks, prior_factor, steering):
    table = dft_table(cube.shape[2] * lax.axis_size("dop"))
    pulse_block = lax.all_to_all(cube, "dop", split_axis=3, concat_axis=2, tiled=True)
    spectrum = lax.all_to_all(
        spectra(pulse_block, table), "dop", split_axis=2, concat_axis=3, tiled=True
    )
    neighbor = from_behind(spectrum[:, :, 0:1, :], "dop", -1)
    following = jnp.concatenate([spectrum[:, :, 1:, :], neighbor], axis=2)
    vectors = jnp.concatenate([spectrum[0], following[0], spectrum[1], following[1]], axis=0)
    usable = train_blocks * guard_blocks[None, :]
    gate_mask = jnp.repeat(usable, BLOCK, axis=1).astype(jnp.bfloat16)
    masked = vectors * gate_mask[None, :, :]
    gram = jnp.einsum("dkg,ekg->kde", masked, masked, preferred_element_type=jnp.float32)
    half = vectors.shape[0] // 2
    real_part = gram[:, :half, :half] + gram[:, half:, half:]
    cross = gram[:, half:, :half] - gram[:, :half, half:]
    prior_gram = forgetting * jnp.einsum(
        "krd,kre->kde", prior_factor, prior_factor, precision=lax.Precision.HIGHEST
    )
    top = jnp.concatenate([real_part, -cross], axis=2)
    bottom = jnp.concatenate([cross, real_part], axis=2)
    local = jnp.concatenate([top, bottom], axis=1) + prior_gram
    covariance = lax.psum(local, "rng")
    lower = jnp.linalg.cholesky(covariance)
    first = lax.linalg.triangular_solve(lower, steering[:, :, None], left_side=True, lower=True)
    second = lax.linalg.triangular_solve(lower, first, left_side=True, lower=True, transpose_a=True)
    weight = second[:, :, 0] / jnp.sum(first[:, :, 0] * first[:, :, 0], axis=1, keepdims=True)
    rotated = jnp.concatenate([-weight[:, half:], weight[:, :half]], axis=1)
    stacked = jnp.stack([weight, rotated]).astype(jnp.bfloat16)
    filtered = jnp.einsum("skd,dkg->skg", stacked, vectors, preferred_element_type=jnp.float32)
    rows = prior_factor.shape[1]
    start = lax.axis_index("rng") * rows
    factor = lax.dynamic_slice_in_dim(jnp.swapaxes(lower, 1, 2), start, rows, axis=1)
    return (filtered, factor)


def solution(mesh):
    return jax.shard_map(
        shards,
        mesh=mesh,
        in_specs=(
            P(None, None, "dop", "rng"),
            P("dop", "rng"),
            P("rng"),
            P("dop", "rng", None),
            P("dop", None),
        ),
        out_specs=(P(None, "dop", "rng"), P("dop", "rng", None)),
        check_vma=False,
    )
```

profile of v0, /device:TPU:64, one launch (start us, length us, event | category | flops | bytes accessed | tf_op | source)
XLA Modules:
  0.0 741.5 jit_solution(6532343640095411719)
XLA Ops:
  7.2 4.0 copy.72
  11.2 2.2 reshape.203
  13.4 10.0 %all-to-all-start = ((bf16[16,2,16384]{2,1,0:T(2,128)(2,1)}), bf16[16,2,16384]{2,1,0:T(2,128)(2,1)S(1)}, u32[]{:S(2)}, u32[]{:S(2)}) async-start(bf16[16,2,16384]{2,1,0:T(2,128)(2,1)} %reshape.203), calls=%async_computation | async-start | bytes 2097152 | tf_op jit(solution)/shard_map/all_to_all | solution.py:37
  24.0 24.0 %all-to-all-done = bf16[16,2,16384]{2,1,0:T(2,128)(2,1)S(1)} async-done(((bf16[16,2,16384]{2,1,0:T(2,128)(2,1)}), bf16[16,2,16384]{2,1,0:T(2,128)(2,1)S(1)}, u32[]{:S(2)}, u32[]{:S(2)}) %all-to-all-start) | async-done | bytes 1048608 | tf_op jit(solution)/shard_map/all_to_all | solution.py:37
  49.4 1.9 copy.74
  51.3 2.9 copy.75
  55.1 3.0 copy.76
  58.2 2.2 reshape.205
  60.4 6.8 all-to-all-start.1
  67.6 24.2 %all-to-all-done.1 = bf16[16,2,16384]{2,1,0:T(2,128)(2,1)S(1)} async-done(((bf16[16,2,16384]{2,1,0:T(2,128)(2,1)}), bf16[16,2,16384]{2,1,0:T(2,128)(2,1)S(1)}, u32[]{:S(2)}, u32[]{:S(2)}) %all-to-all-start.1) | async-done | bytes 1048608 | tf_op jit(solution)/shard_map/all_to_all | solution.py:38
  93.2 1.7 copy.77
  95.4 1.3 copy-done.3
  96.9 3.5 collective-permute-start
  100.4 3.1 fusion.42
  103.7 1.5 copy.118
  107.3 1.4 fusion.7
  108.8 1.5 fusion.1
  110.5 3.3 maximum_add_fusion
  114.6 164.1 %all-reduce.3.cloned.1.call-done = f32[8,256,256]{1,2,0:T(8,128)} async-done(((f32[8,256,256]{1,2,0:T(8,128)}), f32[8,256,256]{1,2,0:T(8,128)}) %all-reduce.3.cloned.1.call-update) | async-done | bytes 2097168 | tf_op jit(solution)/shard_map/psum | solution.py:57
  278.6 3.1 copy.86
  281.7 1.9 fusion
  283.6 1.3 copy-done.5
  284.9 93.8 %custom-call.18 = f32[8,128,128]{2,1,0:T(8,128)S(1)} custom-call(f32[8,128,128]{2,1,0:T(8,128)S(1)} %cholesky.122), custom_call_target="Cholesky" | custom-call | tf_op jit(solution)/shard_map/jit(cholesky)/cholesky | solution.py:58
  379.0 79.4 %custom-call.19 = f32[8,1,128,128]{2,3,1,0:T(8,128)} custom-call(f32[8,1,128,128]{3,2,1,0:T(8,128)S(1)} %select_bitcast_fusion), custom_call_target="InvertDiagBlocksLowerTriangular" | custom-call | tf_op jit(solution)/shard_map/jit(cholesky)/cholesky | solution.py:58
  458.4 1.8 constant_dynamic-update-slice_fusion.1
  460.2 3.1 convolution_subtract_fusion
  463.3 94.6 %custom-call.20 = f32[8,128,128]{2,1,0:T(8,128)S(1)} custom-call(f32[8,128,128]{2,1,0:T(8,128)} %convolution_subtract_fusion), custom_call_target="Cholesky" | custom-call | tf_op jit(solution)/shard_map/jit(cholesky)/cholesky | solution.py:58
  559.3 3.4 broadcast_select_fusion
  562.8 5.8 while.1
  563.4 2.3 bitcast_dynamic-update-slice_fusion.2
  566.3 2.3 bitcast_dynamic-update-slice_fusion.2
  568.7 158.3 %custom-call.21 = f32[8,2,128,128]{2,3,1,0:T(8,128)S(1)} custom-call(f32[8,2,128,128]{3,2,1,0:T(8,128)} %bitcast.155), custom_call_target="InvertDiagBlocksLowerTriangular" | custom-call | tf_op jit(solution)/shard_map/triangular_solve | solution.py:60
  (91 shorter events, 19.0 us)
Async XLA Ops:
  7.2 103.3 %copy-start = (f32[8,8,256]{2,1,0:T(8,128)S(1)}, f32[8,8,256]{2,1,0:T(8,128)}, u32[]{:S(2)}) copy-start(f32[8,8,256]{2,1,0:T(8,128)} %param.8) | copy-start | bytes 196612
  13.4 34.6 %all-to-all-start = ((bf16[16,2,16384]{2,1,0:T(2,128)(2,1)}), bf16[16,2,16384]{2,1,0:T(2,128)(2,1)S(1)}, u32[]{:S(2)}, u32[]{:S(2)}) async-start(bf16[16,2,16384]{2,1,0:T(2,128)(2,1)} %reshape.203), calls=%async_computation | async-start | bytes 2097152 | tf_op jit(solution)/shard_map/all_to_all | solution.py:37
  58.1 9.3 %copy-start.16 = (s32[8,4]{0,1:T(4,128)S(1)}, s32[8,4]{0,1:T(4,128)}, u32[]{:S(2)}) copy-start(s32[8,4]{0,1:T(4,128)} %param.6) | copy-start | bytes 388
  58.2 9.3 %copy-start.17 = (s32[4]{0:T(128)S(1)}, s32[4]{0:T(128)}, u32[]{:S(2)}) copy-start(s32[4]{0:T(128)} %param.7) | copy-start | bytes 52
  60.4 31.4 %all-to-all-start.1 = ((bf16[16,2,16384]{2,1,0:T(2,128)(2,1)}), bf16[16,2,16384]{2,1,0:T(2,128)(2,1)S(1)}, u32[]{:S(2)}, u32[]{:S(2)}) async-start(bf16[16,2,16384]{2,1,0:T(2,128)(2,1)} %reshape.205), calls=%async_computation.1 | async-start | bytes 2097152 | tf_op jit(solution)/shard_map/all_to_all | solution.py:38
  67.2 211.4 %all-reduce.3.cloned.1.call-start = ((), (), s32[]{:S(2)}) async-start(), calls=%async_computation.2 | async-start | bytes 4194304 | tf_op jit(solution)/shard_map/psum | solution.py:57
  95.4 1.3 copy-start.3
  96.9 10.4 %collective-permute-start = (bf16[2,64,1,512]{3,1,2,0:T(8,128)(2,1)S(1)}, bf16[2,64,1,512]{3,1,2,0:T(8,128)(2,1)S(1)}, u32[]{:S(2)}, u32[]{:S(2)}) collective-permute-start(bf16[2,64,1,512]{3,1,2,0:T(8,128)(2,1)S(1)} %copy.119), channel_id=1, source_target_pairs={{32,0},{64,32},{96,64},{128,96},{160,128},{192,160},{224,192},{256... | collective-permute-start | bytes 393224 | tf_op jit(solution)/shard_map/ppermute | solution.py:14
  100.4 3.2 copy-start.4
  106.9 1.9 copy-start.7
  107.3 3.0 copy-start.9
  108.8 1.5 copy-start.11
  108.8 1.5 copy-start.13
  113.8 0.7 copy-start.15
  278.6 3.1 copy-start.1
  283.6 1.3 copy-start.5
  558.0 1.3 copy-start.2
  726.9 4.9 copy-start.8
  726.9 4.9 copy-start.10
  726.9 4.9 copy-start.12
  726.9 4.9 copy-start.14
  731.8 1.6 copy-start.6
Sparse Core Ops, SparseCore 0:
  113.9 164.6 all-reduce.2
where the time goes:
time: 742 us
  other arithmetic  434 us (58%)
  waiting for transfers between devices  212 us (29%)
  local copies, waits for them, and re-layouts  44.3 us (6%)
  starting transfers between devices  20.5 us (3%)
  matrix products  15.5 us (2%)
  between operations  14.5 us (2%)
    another operation x10, other arithmetic, shards(): lower = jnp.linalg.cholesky(covariance)  268 us
    psum x1, waiting for transfers between devices, shards(): covariance = lax.psum(local, 'rng')  164 us
    another operation x5, other arithmetic, shards(): lax.linalg.triangular_solve(lower, first, left_side=True, lower=True, tra...  162 us
    all_to_all x1, waiting for transfers between devices, shards(): lax.all_to_all(spectra(pulse_block, table), 'dop', split_axis=2, concat_a...  24.2 us
    all_to_all x1, waiting for transfers between devices, shards(): lax.all_to_all(cube, 'dop', split_axis=3, concat_axis=2, tiled=True)  24 us
    unnamed x45, local copies, waits for them, and re-layouts  19.4 us
  transfers between devices with their start and end apart: 4, of which 3 were waited for; matrix products, arithmetic and copies ran while one was open for 1% of the time, Pallas kernels for 0%

commit v1 on v0

--- a/solution.py
+++ b/solution.py
@@ -54,7 +54,13 @@
     top = jnp.concatenate([real_part, -cross], axis=2)
     bottom = jnp.concatenate([cross, real_part], axis=2)
     local = jnp.concatenate([top, bottom], axis=1) + prior_gram
-    covariance = lax.psum(local, "rng")
+    n_dev = lax.axis_size("rng")
+    covariance, far = (local, 1)
+    while far < n_dev:
+        covariance = covariance + lax.ppermute(
+            covariance, "rng", [(i_2, i_2 ^ far) for i_2 in range(n_dev)]
+        )
+        far = 2 * far
     lower = jnp.linalg.cholesky(covariance)
     first = lax.linalg.triangular_solve(lower, steering[:, :, None], left_side=True, lower=True)
     second = lax.linalg.triangular_solve(lower, first, left_side=True, lower=True, transpose_a=True)

time: 742 us -> 907 us (1.22)
  the two profiles are of different devices: /device:TPU:64 before, /device:TPU:56 now
where the time goes in v1:
time: 907 us; the launch traced here: 906 us
  other arithmetic  438 us (48%)
  waiting for transfers between devices  374 us (41%)
  local copies, waits for them, and re-layouts  42.4 us (5%)
  starting transfers between devices  36.5 us (4%)
  matrix products  14.2 us (2%)
    ppermute x5, waiting for transfers between devices, shards(): lax.ppermute(covariance, 'rng', [(i_2, i_2 ^ far) for i_2 in range(n_dev)])  322 us
    another operation x10, other arithmetic, shards(): lower = jnp.linalg.cholesky(covariance)  268 us
    another operation x5, other arithmetic, shards(): lax.linalg.triangular_solve(lower, first, left_side=True, lower=True, tra...  161 us
    all_to_all x1, waiting for transfers between devices, shards(): lax.all_to_all(spectra(pulse_block, table), 'dop', split_axis=2, concat_a...  26.3 us
    all_to_all x1, waiting for transfers between devices, shards(): lax.all_to_all(cube, 'dop', split_axis=3, concat_axis=2, tiled=True)  25.9 us
    ppermute x5, starting transfers between devices, shards(): lax.ppermute(covariance, 'rng', [(i_2, i_2 ^ far) for i_2 in range(n_dev)])  20.4 us
    unnamed x47, local copies, waits for them, and re-layouts  18.8 us
  transfers between devices with their start and end apart: 8, of which 7 were waited for; matrix products, arithmetic and copies ran while one was open for 1% of the time, Pallas kernels for 0%

profile of v1, /device:TPU:56, one launch (start us, length us, event | category | flops | bytes accessed | tf_op | source)
XLA Modules:
  0.0 906.2 jit_solution(13544701861242480445)
XLA Ops:
  0.6 4.0 copy.72
  4.7 2.3 reshape.203
  6.9 10.4 %all-to-all-start = ((bf16[16,2,16384]{2,1,0:T(2,128)(2,1)}), bf16[16,2,16384]{2,1,0:T(2,128)(2,1)S(1)}, u32[]{:S(2)}, u32[]{:S(2)}) async-start(bf16[16,2,16384]{2,1,0:T(2,128)(2,1)} %reshape.203), calls=%async_computation | async-start | bytes 2097152 | tf_op jit(solution)/shard_map/all_to_all | solution.py:37
  17.9 25.9 %all-to-all-done = bf16[16,2,16384]{2,1,0:T(2,128)(2,1)S(1)} async-done(((bf16[16,2,16384]{2,1,0:T(2,128)(2,1)}), bf16[16,2,16384]{2,1,0:T(2,128)(2,1)S(1)}, u32[]{:S(2)}, u32[]{:S(2)}) %all-to-all-start) | async-done | bytes 1048608 | tf_op jit(solution)/shard_map/all_to_all | solution.py:37
  45.2 1.9 copy.74
  47.0 2.9 copy.75
  50.9 3.0 copy.76
  53.9 2.3 reshape.205
  56.2 4.9 all-to-all-start.1
  61.3 26.3 %all-to-all-done.1 = bf16[16,2,16384]{2,1,0:T(2,128)(2,1)S(1)} async-done(((bf16[16,2,16384]{2,1,0:T(2,128)(2,1)}), bf16[16,2,16384]{2,1,0:T(2,128)(2,1)S(1)}, u32[]{:S(2)}, u32[]{:S(2)}) %all-to-all-start.1) | async-done | bytes 1048608 | tf_op jit(solution)/shard_map/all_to_all | solution.py:38
  93.4 3.2 fusion.42
  103.6 2.0 maximum_add_fusion
  105.5 3.2 collective-permute-start.1
  108.8 46.9 %collective-permute-done.1 = f32[8,256,256]{1,2,0:T(8,128)S(1)} collective-permute-done((f32[8,256,256]{1,2,0:T(8,128)S(1)}, f32[8,256,256]{1,2,0:T(8,128)S(1)}, u32[]{:S(2)}, u32[]{:S(2)}) %collective-permute-start.1) | collective-permute-done | bytes 2097184 | tf_op jit(solution)/shard_map/ppermute | solution.py:60
  156.0 4.0 collective-permute-start.2
  160.0 91.3 %collective-permute-done.2 = f32[8,256,256]{1,2,0:T(8,128)S(1)} collective-permute-done((f32[8,256,256]{1,2,0:T(8,128)S(1)}, f32[8,256,256]{1,2,0:T(8,128)S(1)}, u32[]{:S(2)}, u32[]{:S(2)}) %collective-permute-start.2) | collective-permute-done | bytes 2097184 | tf_op jit(solution)/shard_map/ppermute | solution.py:60
  251.7 4.6 collective-permute-start.3
  256.3 92.9 %collective-permute-done.3 = f32[8,256,256]{1,2,0:T(8,128)S(1)} collective-permute-done((f32[8,256,256]{1,2,0:T(8,128)S(1)}, f32[8,256,256]{1,2,0:T(8,128)S(1)}, u32[]{:S(2)}, u32[]{:S(2)}) %collective-permute-start.3) | collective-permute-done | bytes 2097184 | tf_op jit(solution)/shard_map/ppermute | solution.py:60
  349.5 3.4 collective-permute-start.4
  352.9 46.0 %collective-permute-done.4 = f32[8,256,256]{1,2,0:T(8,128)S(1)} collective-permute-done((f32[8,256,256]{1,2,0:T(8,128)S(1)}, f32[8,256,256]{1,2,0:T(8,128)S(1)}, u32[]{:S(2)}, u32[]{:S(2)}) %collective-permute-start.4) | collective-permute-done | bytes 2097184 | tf_op jit(solution)/shard_map/ppermute | solution.py:60
  399.2 5.1 collective-permute-start.5
  404.5 44.8 %collective-permute-done.5 = f32[8,256,256]{1,2,0:T(8,128)} collective-permute-done((f32[8,256,256]{1,2,0:T(8,128)S(1)}, f32[8,256,256]{1,2,0:T(8,128)}, u32[]{:S(2)}, u32[]{:S(2)}) %collective-permute-start.5) | collective-permute-done | bytes 2097184 | tf_op jit(solution)/shard_map/ppermute | solution.py:60
  449.3 2.6 add.82
  457.0 93.8 %custom-call.18 = f32[8,128,128]{2,1,0:T(8,128)S(1)} custom-call(f32[8,128,128]{2,1,0:T(8,128)S(1)} %cholesky.122), custom_call_target="Cholesky" | custom-call | tf_op jit(solution)/shard_map/jit(cholesky)/cholesky | solution.py:64
  551.0 79.2 %custom-call.19 = f32[8,1,128,128]{2,3,1,0:T(8,128)} custom-call(f32[8,1,128,128]{3,2,1,0:T(8,128)S(1)} %select_bitcast_fusion), custom_call_target="InvertDiagBlocksLowerTriangular" | custom-call | tf_op jit(solution)/shard_map/jit(cholesky)/cholesky | solution.py:64
  632.1 3.1 slice_subtract_fusion
  635.1 94.6 %custom-call.20 = f32[8,128,128]{2,1,0:T(8,128)S(1)} custom-call(f32[8,128,128]{2,1,0:T(8,128)} %slice_subtract_fusion), custom_call_target="Cholesky" | custom-call | tf_op jit(solution)/shard_map/jit(cholesky)/cholesky | solution.py:64
  731.1 3.4 broadcast_select_fusion
  734.6 5.8 while.1
  735.2 2.3 bitcast_dynamic-update-slice_fusion.2
  738.1 2.3 bitcast_dynamic-update-slice_fusion.2
  740.4 158.0 %custom-call.21 = f32[8,2,128,128]{2,3,1,0:T(8,128)S(1)} custom-call(f32[8,2,128,128]{3,2,1,0:T(8,128)} %bitcast.155), custom_call_target="InvertDiagBlocksLowerTriangular" | custom-call | tf_op jit(solution)/shard_map/triangular_solve | solution.py:66
  (105 shorter events, 34.3 us)
Async XLA Ops:
  0.6 102.9 %copy-start = (f32[8,8,256]{2,1,0:T(8,128)S(1)}, f32[8,8,256]{2,1,0:T(8,128)}, u32[]{:S(2)}) copy-start(f32[8,8,256]{2,1,0:T(8,128)} %param.8) | copy-start | bytes 196612
  6.9 36.9 %all-to-all-start = ((bf16[16,2,16384]{2,1,0:T(2,128)(2,1)}), bf16[16,2,16384]{2,1,0:T(2,128)(2,1)S(1)}, u32[]{:S(2)}, u32[]{:S(2)}) async-start(bf16[16,2,16384]{2,1,0:T(2,128)(2,1)} %reshape.203), calls=%async_computation | async-start | bytes 2097152 | tf_op jit(solution)/shard_map/all_to_all | solution.py:37
  53.9 7.2 copy-start.17
  53.9 7.2 copy-start.18
  56.2 31.4 %all-to-all-start.1 = ((bf16[16,2,16384]{2,1,0:T(2,128)(2,1)}), bf16[16,2,16384]{2,1,0:T(2,128)(2,1)S(1)}, u32[]{:S(2)}, u32[]{:S(2)}) async-start(bf16[16,2,16384]{2,1,0:T(2,128)(2,1)} %reshape.205), calls=%async_computation.1 | async-start | bytes 2097152 | tf_op jit(solution)/shard_map/all_to_all | solution.py:38
  91.2 1.3 copy-start.4
  92.7 7.7 collective-permute-start
  93.4 3.2 copy-start.5
  99.9 1.9 copy-start.8
  100.4 3.0 copy-start.10
  101.8 1.5 copy-start.12
  101.8 1.5 copy-start.14
  105.5 50.2 %collective-permute-start.1 = (f32[8,256,256]{1,2,0:T(8,128)S(1)}, f32[8,256,256]{1,2,0:T(8,128)S(1)}, u32[]{:S(2)}, u32[]{:S(2)}) collective-permute-start(f32[8,256,256]{1,2,0:T(8,128)S(1)} %maximum_add_fusion), channel_id=1, source_target_pairs={{0,1},{1,0},{2,3},{3,2},{4,5},{5,4},{6,7},{7,6},{8,9},{9,8},{10,11... | collective-permute-start | bytes 6291464 | tf_op jit(solution)/shard_map/ppermute | solution.py:60
  156.0 95.4 %collective-permute-start.2 = (f32[8,256,256]{1,2,0:T(8,128)S(1)}, f32[8,256,256]{1,2,0:T(8,128)S(1)}, u32[]{:S(2)}, u32[]{:S(2)}) collective-permute-start(f32[8,256,256]{1,2,0:T(8,128)S(1)} %add.78), channel_id=1, source_target_pairs={{0,2},{1,3},{2,0},{3,1},{4,6},{5,7},{6,4},{7,5},{8,10},{9,11},{10,... | collective-permute-start | bytes 6291464 | tf_op jit(solution)/shard_map/ppermute | solution.py:60
  251.7 97.5 %collective-permute-start.3 = (f32[8,256,256]{1,2,0:T(8,128)S(1)}, f32[8,256,256]{1,2,0:T(8,128)S(1)}, u32[]{:S(2)}, u32[]{:S(2)}) collective-permute-start(f32[8,256,256]{1,2,0:T(8,128)S(1)} %add.79), channel_id=1, source_target_pairs={{0,4},{1,5},{2,6},{3,7},{4,0},{5,1},{6,2},{7,3},{8,12},{9,13},{10,... | collective-permute-start | bytes 6291464 | tf_op jit(solution)/shard_map/ppermute | solution.py:60
  349.5 54.9 %copy-start.16 = (f32[8,256]{1,0:T(8,128)S(1)}, f32[8,256]{1,0:T(8,128)}, u32[]{:S(2)}) copy-start(f32[8,256]{1,0:T(8,128)} %param.9) | copy-start | bytes 24580
  349.5 49.4 %collective-permute-start.4 = (f32[8,256,256]{1,2,0:T(8,128)S(1)}, f32[8,256,256]{1,2,0:T(8,128)S(1)}, u32[]{:S(2)}, u32[]{:S(2)}) collective-permute-start(f32[8,256,256]{1,2,0:T(8,128)S(1)} %add.80), channel_id=1, source_target_pairs={{0,8},{1,9},{2,10},{3,11},{4,12},{5,13},{6,14},{7,15},{8,0},{9,1},... | collective-permute-start | bytes 6291464 | tf_op jit(solution)/shard_map/ppermute | solution.py:60
  399.2 5.3 copy-start.2
  399.2 50.1 %collective-permute-start.5 = (f32[8,256,256]{1,2,0:T(8,128)S(1)}, f32[8,256,256]{1,2,0:T(8,128)}, u32[]{:S(2)}, u32[]{:S(2)}) collective-permute-start(f32[8,256,256]{1,2,0:T(8,128)S(1)} %add.81), channel_id=1, source_target_pairs={{0,16},{1,17},{2,18},{3,19},{4,20},{5,21},{6,22},{7,23},{8,24},{9,... | collective-permute-start | bytes 6291464 | tf_op jit(solution)/shard_map/ppermute | solution.py:60
  455.6 1.3 copy-start.6
  729.8 1.3 copy-start.3
  898.4 4.9 copy-start.9
  898.4 4.9 copy-start.11
  898.4 4.9 copy-start.13
  898.4 4.9 copy-start.15
  903.3 1.6 copy-start.7
  903.3 2.9 copy-start.1
